TPU v7x, 32 devices: a whole 2x2x4 slice. The times are simulated.
32 devices in a mesh: fsdp: 4 (over y, x), grp: 8 (over z, core).
Axes of the slice: x: 2, y: 2, z: 4, core: 2. Of those that a mesh axis runs over, the one named last changes fastest.
Arguments:
- grad_out: bfloat16 [32, 512, 512], P(('fsdp', 'grp')), may hold values from -6 to 6
- pre_first: bfloat16 [32, 512, 512], P(('fsdp', 'grp')), may hold values from -8 to 8
- pre_second: bfloat16 [32, 512, 512], P(('fsdp', 'grp')), may hold values from -8 to 8
- conv_first: bfloat16 [3, 512, 512], P(None, 'fsdp'), may hold values from -0.15625 to 0.15625
- conv_second: bfloat16 [3, 512, 512], P(None, 'fsdp'), may hold values from -0.15625 to 0.15625
- lengths: int32 [32], P(('fsdp', 'grp')), may hold values from 64 to 512
- item_ids: int32 [16384], P('grp'), may hold values from 0 to 8191
- owners: int32 [512, 1], P('grp'), may hold values from 0 to 7; in each aligned block of 64 rows (0 to 63, 64 to 127, ...) at most 16 rows name the same one
Outputs:
- table_grad: float32 [512, 65536], P('fsdp', 'grp')
Inputs may be any that keep to these rules, and one draw needn't show every extreme that they name: `owners`: among the blocks of one group, no owner is named by more than 16 blocks, a bound that some block reaches.
All inputs are finite; a program needn't handle non-finite values.
Results may differ from a plain program's by a relative error of at most 0.0037.
Values may be sent and summed in bfloat16 or wider, within the bound.
A program may use at most 64 MiB of HBM per device.

v0:
```python
import jax
import jax.numpy as jnp
from jax import lax
from jax.sharding import PartitionSpec as P

BLK = 32
ROWS_OWN = 8192


def layer_back(gradient, pre_acts, live_rows, dilation, product):
    seq_len = gradient.shape[0]
    pre_float = pre_acts.astype(jnp.float32)
    sig_val = jax.nn.sigmoid(pre_float)
    deltas = (gradient * sig_val * (1.0 + pre_float * (1.0 - sig_val))).astype(jnp.bfloat16)
    padded = jnp.pad(deltas, ((dilation, dilation), (0, 0)))
    tap_rows = jnp.stack(
        [
            padded[2 * dilation : 2 * dilation + seq_len],
            padded[dilation : dilation + seq_len],
            padded[0:seq_len],
        ]
    )
    return gradient + live_rows * product(tap_rows)


def gathered_product(weights):

    def apply_taps(tap_rows):
        return jnp.einsum(
            "ktd,kpd->tp",
            tap_rows,
            lax.all_gather(weights, "fsdp", axis=1, tiled=True),
            preferred_element_type=jnp.float32,
        )

    return apply_taps


def body(grad_out, pre_first, pre_second, conv_first, conv_second, lengths, item_ids, owners):
    seq_len = grad_out.shape[1]
    positions = jnp.arange(seq_len, dtype=jnp.int32)
    live_rows = (positions < lengths[0]).astype(jnp.float32)[:, None]
    gradient = grad_out[0].astype(jnp.float32)
    gradient = layer_back(gradient, pre_second[0], live_rows, 2, gathered_product(conv_second))
    gradient = layer_back(gradient, pre_first[0], live_rows, 1, gathered_product(conv_first))
    row_grad = (live_rows * gradient).astype(jnp.bfloat16)
    group_cols = lax.all_to_all(row_grad.T, "fsdp", split_axis=0, concat_axis=1, tiled=True)
    feat_cols = group_cols.shape[0]
    owner_count = lax.axis_size("grp")
    blocks = owners.shape[0]
    slot_cap = max(2, 2 * blocks // owner_count)
    block_dest = owners[:, 0]
    dest_hits = (block_dest[:, None] == jnp.arange(owner_count, dtype=jnp.int32)[None, :]).astype(
        jnp.int32
    )
    earlier = jnp.cumsum(dest_hits, axis=0) - dest_hits
    block_rank = jnp.sum(dest_hits * earlier, axis=1)
    slot_index = block_dest * slot_cap + block_rank
    select_int = (
        slot_index[:, None] == jnp.arange(owner_count * slot_cap, dtype=jnp.int32)[None, :]
    ).astype(jnp.int32)
    select_int = select_int.reshape(blocks, owner_count, slot_cap)
    select_map = select_int.astype(jnp.bfloat16)
    block_cols = group_cols.reshape(feat_cols, blocks, BLK)
    send_rows = jnp.einsum(
        "cbr,bos->ocsr", block_cols, select_map, preferred_element_type=jnp.float32
    )
    send_rows = send_rows.astype(jnp.bfloat16).reshape(owner_count, feat_cols, slot_cap * BLK)
    shifted_ids = item_ids.reshape(blocks, BLK) + 1
    send_ids = jnp.einsum("br,bos->osr", shifted_ids, select_int) - 1
    send_ids = send_ids.reshape(owner_count, slot_cap * BLK)
    recv_rows, recv_ids = (
        lax.all_to_all(send_rows, "grp", split_axis=0, concat_axis=0, tiled=True),
        lax.all_to_all(send_ids, "grp", split_axis=0, concat_axis=0, tiled=True),
    )
    flat_rows = jnp.transpose(recv_rows, (0, 2, 1)).reshape(-1, feat_cols).astype(jnp.float32)
    safe_ids = jnp.where(recv_ids < 0, ROWS_OWN, recv_ids).reshape(-1)
    summed = jax.ops.segment_sum(flat_rows, safe_ids, num_segments=ROWS_OWN + 1)
    return summed[:ROWS_OWN].T


def solution(mesh):
    placed = (
        P(("fsdp", "grp"), None, None),
        P(("fsdp", "grp"), None, None),
        P(("fsdp", "grp"), None, None),
        P(None, "fsdp", None),
        P(None, "fsdp", None),
        P(("fsdp", "grp")),
        P("grp"),
        P("grp", None),
    )
    return jax.shard_map(
        body, mesh=mesh, in_specs=placed, out_specs=P("fsdp", "grp"), check_vma=False
    )
```

profile of v0, /device:TPU:0, one launch (start us, length us, event | category | flops | bytes accessed | tf_op | source)
XLA Modules:
  0.0 175.9 jit_solution(7663716986740653124)
XLA Ops:
  6.5 0.7 all-gather.3.cloned.1.call-update
  7.3 0.0 all-gather.5.cloned.1.call-start
  7.3 0.7 all-gather.5.cloned.1.call-update
  8.7 0.7 fusion.74
  9.4 0.1 reduce_window_sum.11
  9.5 0.8 select_reduce_fusion
  10.3 0.0 copy-start.2
  10.3 0.0 copy-start
  10.4 1.7 fusion.46
  12.1 0.2 slice_bitcast_fusion.4
  12.4 0.5 fusion.48
  12.8 30.0 %all-gather.3.cloned.1.call-done = bf16[3,512,512]{2,1,0:T(8,128)(2,1)} async-done(((bf16[3,128,512]{2,1,0:T(8,128)(2,1)}), bf16[3,512,512]{2,1,0:T(8,128)(2,1)}) %all-gather.3.cloned.1.call-update) | async-done | bytes 1572880 | tf_op jit(solution)/shard_map/all_gather | solution.py:32
  42.8 3.7 %fusion.54 = (bf16[512,512]{1,0:T(8,128)(2,1)S(1)}, f32[512,512]{1,0:T(8,128)}) fusion(bf16[1,512,512]{2,1,0:T(8,128)(2,1)S(1)} %copy-done.4, bf16[3,512,512]{2,1,0:T(8,128)(2,1)} %all-gather.3.cloned.1.call-done, bf16[1,512,512]{2,1,0:T(8,128)(2,1)S(1)} %get-tuple-element.8, bf16[1,512,512]{2,1,0:T(8,128)(2,1)S(1)} %fusion.48, ...), kind=kOutput, calls=%fused_computation.47 | convolution fusion | flops 810287104 | bytes 5769216 | tf_op jit(solution)/shard_map/ktd,kpd->tp/dot_general | solution.py:29
  46.4 0.2 slice_bitcast_fusion.2
  46.7 28.8 %all-gather.5.cloned.1.call-done = bf16[3,512,512]{2,1,0:T(8,128)(2,1)} async-done(((bf16[3,128,512]{2,1,0:T(8,128)(2,1)}), bf16[3,512,512]{2,1,0:T(8,128)(2,1)}) %all-gather.5.cloned.1.call-update) | async-done | bytes 1572880 | tf_op jit(solution)/shard_map/all_gather | solution.py:32
  75.5 2.4 %fusion.42 = bf16[64,4,8,128]{3,2,1,0:T(8,128)(2,1)S(1)} fusion(f32[512,512]{1,0:T(8,128)S(1)} %copy-done.5, bf16[3,512,512]{2,1,0:T(8,128)(2,1)} %all-gather.5.cloned.1.call-done, bf16[1,512,512]{2,1,0:T(8,128)(2,1)S(1)} %get-tuple-element.6, bf16[1,512,512]{2,1,0:T(8,128)(2,1)S(1)} %bitcast.101, bf16[1,512,512]{2,1,0:T(8,128)(2,1)S(1)} %get-tuple-element.5, ...), kind=kOutput, calls=%fused_computation.36 | convolution fusion | flops 807927808 | bytes 4720640 | tf_op jit(solution)/shard_map/ktd,kpd->tp/dot_general | solution.py:29
  77.9 0.9 copy.34
  78.8 3.5 %all-to-all-start.1 = ((bf16[4,128,512]{1,2,0:T(8,128)(2,1)}), bf16[4,128,512]{1,2,0:T(8,128)(2,1)S(1)}, u32[]{:S(2)}, u32[]{:S(2)}) async-start(bf16[4,128,512]{1,2,0:T(8,128)(2,1)} %bitcast.97), calls=%async_computation.1 | async-start | bytes 1048576 | tf_op jit(solution)/shard_map/all_to_all | solution.py:47
  82.3 0.1 add.52
  82.4 0.2 convolution_add_fusion
  82.6 0.7 all_to_all.30
  83.3 7.1 %all-to-all-done.1 = bf16[4,128,512]{1,2,0:T(8,128)(2,1)S(1)} async-done(((bf16[4,128,512]{1,2,0:T(8,128)(2,1)}), bf16[4,128,512]{1,2,0:T(8,128)(2,1)S(1)}, u32[]{:S(2)}, u32[]{:S(2)}) %all-to-all-start.1) | async-done | bytes 524320 | tf_op jit(solution)/shard_map/all_to_all | solution.py:47
  90.4 4.6 %all-to-all-start = ((s32[8,1,512]{2,1,0:T(1,128)}), s32[8,1,512]{2,1,0:T(1,128)S(1)}, u32[]{:S(2)}, u32[]{:S(2)}) async-start(s32[8,1,512]{2,1,0:T(1,128)} %all_to_all.30), calls=%async_computation | async-start | bytes 32768 | tf_op jit(solution)/shard_map/all_to_all | solution.py:74
  95.0 0.5 fusion.14
  95.5 1.2 copy.21
  96.7 3.9 %all-to-all-done = s32[8,1,512]{2,1,0:T(1,128)S(1)} async-done(((s32[8,1,512]{2,1,0:T(1,128)}), s32[8,1,512]{2,1,0:T(1,128)S(1)}, u32[]{:S(2)}, u32[]{:S(2)}) %all-to-all-start) | async-done | bytes 16416 | tf_op jit(solution)/shard_map/all_to_all | solution.py:74
  100.7 3.6 %all-to-all-start.2 = ((bf16[8,128,512]{1,2,0:T(8,128)(2,1)}), bf16[8,128,512]{1,2,0:T(8,128)(2,1)S(1)}, u32[]{:S(2)}, u32[]{:S(2)}) async-start(bf16[8,128,512]{1,2,0:T(8,128)(2,1)} %bitcast.25), calls=%async_computation.2 | async-start | bytes 2097152 | tf_op jit(solution)/shard_map/all_to_all | solution.py:73
  104.2 26.5 %all-to-all-done.2 = bf16[8,128,512]{1,2,0:T(8,128)(2,1)S(1)} async-done(((bf16[8,128,512]{1,2,0:T(8,128)(2,1)}), bf16[8,128,512]{1,2,0:T(8,128)(2,1)S(1)}, u32[]{:S(2)}, u32[]{:S(2)}) %all-to-all-start.2) | async-done | bytes 1048608 | tf_op jit(solution)/shard_map/all_to_all | solution.py:73
  130.7 0.1 convert_element_type.105
  130.9 28.2 %scatter_custom_fusion = f32[8193,128]{1,0:T(8,128)} fusion(s32[4096]{0:T(1024)S(1)} %bitcast.103, f32[4096,128]{1,0:T(8,128)S(1)} %bitcast.99, f32[]{:T(128)} %constant.8.clone.1), kind=kCustom, calls=%fused_computation.2 | custom fusion | flops 524288 | bytes 4194820 | tf_op jit(solution)/shard_map/scatter-add | solution.py:78
  159.1 4.4 %slice_bitcast_fusion = f32[128,8192]{0,1:T(8,128)} fusion(f32[8193,128]{1,0:T(8,128)} %scatter_custom_fusion), kind=kLoop, calls=%fused_computation.1 | loop fusion | bytes 8388608 | tf_op jit(solution)/shard_map/transpose | solution.py:79
  163.5 5.6 %copy.22 = f32[128,8192]{1,0:T(8,128)} copy(f32[128,8192]{0,1:T(8,128)} %slice_bitcast_fusion) | data formatting | bytes 8388608 | tf_op jit(solution)/shard_map/transpose | solution.py:79
  (16 shorter events, 0.1 us)
Async XLA Ops:
  6.5 36.2 %all-gather.3.cloned.1.call-start = ((), (), s32[]{:S(2)}) async-start(), calls=%async_computation.3 | async-start | bytes 1966080 | tf_op jit(solution)/shard_map/all_gather | solution.py:32
  7.3 68.2 %all-gather.5.cloned.1.call-start = ((), (), s32[]{:S(2)}) async-start(), calls=%async_computation.4 | async-start | bytes 1966080 | tf_op jit(solution)/shard_map/all_gather | solution.py:32
  10.3 2.0 %copy-start.2 = (s32[2048]{0:T(1024)S(1)}, s32[2048]{0:T(1024)}, u32[]{:S(2)}) copy-start(s32[2048]{0:T(1024)} %param.14) | copy-start | bytes 24580
  10.3 2.0 %copy-start = (bf16[1,512,512]{2,1,0:T(8,128)(2,1)S(1)}, bf16[1,512,512]{2,1,0:T(8,128)(2,1)}, u32[]{:S(2)}) copy-start(bf16[1,512,512]{2,1,0:T(8,128)(2,1)} %param.10) | copy-start | bytes 1572868
  10.3 2.0 %copy-start.1 = (bf16[1,512,512]{2,1,0:T(8,128)(2,1)S(1)}, bf16[1,512,512]{2,1,0:T(8,128)(2,1)}, u32[]{:S(2)}) copy-start(bf16[1,512,512]{2,1,0:T(8,128)(2,1)} %param.8) | copy-start | bytes 1572868
  12.1 30.7 %copy-start.4 = (bf16[1,512,512]{2,1,0:T(8,128)(2,1)S(1)}, bf16[1,512,512]{2,1,0:T(8,128)(2,1)}, u32[]{:S(2)}) copy-start(bf16[1,512,512]{2,1,0:T(8,128)(2,1)} %param.9) | copy-start | bytes 1572868
  46.4 29.0 %copy-start.5 = (f32[512,512]{1,0:T(8,128)S(1)}, f32[512,512]{1,0:T(8,128)}, u32[]{:S(2)}) copy-start(f32[512,512]{1,0:T(8,128)} %get-tuple-element.10) | copy-start | bytes 3145732
  77.9 4.4 %copy-start.3 = (s32[64,1]{0,1:T(1,128)S(1)}, s32[64,1]{0,1:T(1,128)}, u32[]{:S(2)}) copy-start(s32[64,1]{0,1:T(1,128)} %param.15) | copy-start | bytes 772
  78.8 11.6 %all-to-all-start.1 = ((bf16[4,128,512]{1,2,0:T(8,128)(2,1)}), bf16[4,128,512]{1,2,0:T(8,128)(2,1)S(1)}, u32[]{:S(2)}, u32[]{:S(2)}) async-start(bf16[4,128,512]{1,2,0:T(8,128)(2,1)} %bitcast.97), calls=%async_computation.1 | async-start | bytes 1048576 | tf_op jit(solution)/shard_map/all_to_all | solution.py:47
  90.4 10.3 %all-to-all-start = ((s32[8,1,512]{2,1,0:T(1,128)}), s32[8,1,512]{2,1,0:T(1,128)S(1)}, u32[]{:S(2)}, u32[]{:S(2)}) async-start(s32[8,1,512]{2,1,0:T(1,128)} %all_to_all.30), calls=%async_computation | async-start | bytes 32768 | tf_op jit(solution)/shard_map/all_to_all | solution.py:74
  100.7 30.1 %all-to-all-start.2 = ((bf16[8,128,512]{1,2,0:T(8,128)(2,1)}), bf16[8,128,512]{1,2,0:T(8,128)(2,1)S(1)}, u32[]{:S(2)}, u32[]{:S(2)}) async-start(bf16[8,128,512]{1,2,0:T(8,128)(2,1)} %bitcast.25), calls=%async_computation.2 | async-start | bytes 2097152 | tf_op jit(solution)/shard_map/all_to_all | solution.py:73
Sparse Core Ops, SparseCore 0:
  9.2 33.5 all-gather.2
  44.6 30.8 all-gather.4
where the time goes:
time: 176 us
  waiting for transfers between devices  97.7 us (56%)
  other arithmetic  32.2 us (18%)
  between operations  14.2 us (8%)
  local copies, waits for them, and re-layouts  13.4 us (8%)
  starting transfers between devices  11.7 us (7%)
  matrix products  6.8 us (4%)
    all_gather x2, waiting for transfers between devices, apply_taps(): lax.all_gather(weights, 'fsdp', axis=1, tiled=True)  58.8 us
    scatter-add x1, other arithmetic, body(): summed = jax.ops.segment_sum(flat_rows, safe_ids, num_segments=ROWS_OWN + 1)  28.2 us
    all_to_all x1, waiting for transfers between devices, body(): lax.all_to_all(send_rows, 'grp', split_axis=0, concat_axis=0, tiled=True)  26.5 us
    transpose x2, local copies, waits for them, and re-layouts, body(): return summed[:ROWS_OWN].T  10 us
    all_to_all x1, waiting for transfers between devices, body(): lax.all_to_all(row_grad.T, 'fsdp', split_axis=0, concat_axis=1, tiled=True)  7.07 us
    dot_general x2, matrix products, apply_taps(): jnp.einsum('ktd,kpd->tp', tap_rows, lax.all_gather(weights, 'fsdp', axis=...  6.08 us
    all_to_all x1, starting transfers between devices, body(): lax.all_to_all(send_ids, 'grp', split_axis=0, concat_axis=0, tiled=True)  4.6 us
    all_to_all x1, waiting for transfers between devices, body(): lax.all_to_all(send_ids, 'grp', split_axis=0, concat_axis=0, tiled=True)  3.93 us
  transfers between devices with their start and end apart: 5, of which 5 were waited for; matrix products, arithmetic and copies ran while one was open for 6% of the time, Pallas kernels for 0%

commit v1 on v0

--- a/solution.py
+++ b/solution.py
@@ -5,6 +5,28 @@
 
 BLK = 32
 ROWS_OWN = 8192
+
+
+def laid_out(tiles, dim):
+    tiles = jnp.moveaxis(tiles, 0, dim)
+    shape = tiles.shape
+    return tiles.reshape(*shape[:dim], shape[dim] * shape[dim + 1], *shape[dim + 2 :])
+
+
+def gather_around(shard, axis, dim):
+    size = lax.axis_size(axis)
+    pairs = [(i, (i + 1) % size) for i in range(size)]
+    back = [(b, a) for a, b in pairs]
+    lower, upper = ([], [])
+    for lap in range(size - 1):
+        if lap % 2 == 0:
+            lower.append(lax.ppermute(lower[-1] if lower else shard, axis, pairs))
+        else:
+            upper.append(lax.ppermute(upper[-1] if upper else shard, axis, back))
+    blocks = jnp.stack([*lower[::-1], shard, *upper])
+    shift = lax.axis_index(axis) - len(lower)
+    blocks = blocks[(jnp.arange(size) - shift) % size]
+    return laid_out(blocks, dim)
 
 
 def layer_back(gradient, pre_acts, live_rows, dilation, product):
@@ -29,7 +51,7 @@
         return jnp.einsum(
             "ktd,kpd->tp",
             tap_rows,
-            lax.all_gather(weights, "fsdp", axis=1, tiled=True),
+            gather_around(weights, "fsdp", 1),
             preferred_element_type=jnp.float32,
         )
 

time: 176 us -> 154 us (0.88)
  waiting for transfers between devices: 97.7 us -> 74.2 us
  between operations: 14.2 us -> 0.9 us
  starting transfers between devices: 11.7 us -> 20.8 us
  local copies, waits for them, and re-layouts: 13.4 us -> 19.8 us
  matrix products: 6.8 us -> 3.03 us
  other arithmetic: 32.2 us -> 35.2 us
    all_gather x2 -> x0, waiting for transfers between devices: 58.8 us -> none  [apply_taps(): lax.all_gather(weights, 'fsdp', axis=1, tiled=True)]
    ppermute x0 -> x6, waiting for transfers between devices: none -> 37.1 us  [the longest x4 37.1 us: gather_around(): lower.append(lax.ppermute(lower[-1] if lower else shard, axis, pairs))]
    ppermute x0 -> x6, starting transfers between devices: none -> 8.98 us  [the longest x4 6.17 us: gather_around(): lower.append(lax.ppermute(lower[-1] if lower else shard, axis, pairs))]
    dot_general x2, matrix products: 6.08 us -> 2.32 us  [apply_taps(): jnp.einsum('ktd,kpd->tp', tap_rows, gather_around(weights, 'fsdp', 1), pr...]
    unnamed x12 -> x26, local copies, waits for them, and re-layouts: 0.04 us -> 2.68 us
  transfers between devices with their start and end apart: 5 -> 9, of which waited for: 5 -> 7; matrix products, arithmetic and copies ran while one was open for 6% -> 7% of each run, Pallas kernels for 0% -> 0%
where the time goes in v1:
time: 154 us
  waiting for transfers between devices  74.2 us (48%)
  other arithmetic  35.2 us (23%)
  starting transfers between devices  20.8 us (14%)
  local copies, waits for them, and re-layouts  19.8 us (13%)
  matrix products  3.03 us (2%)
    ppermute x4, waiting for transfers between devices, gather_around(): lower.append(lax.ppermute(lower[-1] if lower else shard, axis, pairs))  37.1 us
    scatter-add x1, other arithmetic, body(): summed = jax.ops.segment_sum(flat_rows, safe_ids, num_segments=ROWS_OWN + 1)  28.2 us
    all_to_all x1, waiting for transfers between devices, body(): lax.all_to_all(send_rows, 'grp', split_axis=0, concat_axis=0, tiled=True)  26.5 us
    transpose x2, local copies, waits for them, and re-layouts, body(): return summed[:ROWS_OWN].T  10 us
    all_to_all x1, waiting for transfers between devices, body(): lax.all_to_all(row_grad.T, 'fsdp', split_axis=0, concat_axis=1, tiled=True)  6.65 us
    ppermute x4, starting transfers between devices, gather_around(): lower.append(lax.ppermute(lower[-1] if lower else shard, axis, pairs))  6.17 us
    all_to_all x1, starting transfers between devices, body(): lax.all_to_all(send_ids, 'grp', split_axis=0, concat_axis=0, tiled=True)  4.78 us
    all_to_all x1, waiting for transfers between devices, body(): lax.all_to_all(send_ids, 'grp', split_axis=0, concat_axis=0, tiled=True)  3.93 us
  transfers between devices with their start and end apart: 9, of which 7 were waited for; matrix products, arithmetic and copies ran while one was open for 7% of the time, Pallas kernels for 0%

profile of v1, /device:TPU:0, one launch (start us, length us, event | category | flops | bytes accessed | tf_op | source)
XLA Modules:
  0.0 153.9 jit_solution(12950307782741568837)
XLA Ops:
  0.0 3.0 %collective-permute-start.3 = (bf16[3,128,512]{2,1,0:T(8,128)(2,1)}, bf16[3,128,512]{2,1,0:T(8,128)(2,1)S(1)}, u32[]{:S(2)}, u32[]{:S(2)}) collective-permute-start(bf16[3,128,512]{2,1,0:T(8,128)(2,1)} %param.11), channel_id=1, source_target_pairs={{0,8},{8,16},{16,24},{24,0},{1,9},{9,17},{17,25},{25,1},{2,10},{10... | collective-permute-start | bytes 1179656 | tf_op jit(solution)/shard_map/ppermute | solution.py:23
  3.0 1.0 collective-permute-start.5
  3.9 1.1 collective-permute-start
  5.0 1.9 %collective-permute-start.2 = (bf16[3,128,512]{2,1,0:T(8,128)(2,1)}, bf16[3,128,512]{2,1,0:T(8,128)(2,1)}, u32[]{:S(2)}, u32[]{:S(2)}) collective-permute-start(bf16[3,128,512]{2,1,0:T(8,128)(2,1)} %param.12), channel_id=1, source_target_pairs={{8,0},{16,8},{24,16},{0,24},{9,1},{17,9},{25,17},{1,25},{10,2},{18... | collective-permute-start | bytes 1179656 | tf_op jit(solution)/shard_map/ppermute | solution.py:25
  7.5 0.7 fusion.74
  8.3 1.4 select_reduce_fusion
  9.8 1.7 %fusion.46 = bf16[512,512]{1,0:T(8,128)(2,1)S(1)} fusion(bf16[1,512,512]{2,1,0:T(8,128)(2,1)} %param.8, bf16[1,512,512]{2,1,0:T(8,128)(2,1)} %param.10), kind=kLoop, calls=%fused_computation.43 | loop fusion | flops 2883584 | bytes 1572864 | tf_op jit(solution)/shard_map/convert_element_type | solution.py:36
  11.5 1.2 slice_bitcast_fusion.4
  12.7 1.3 fusion.48
  14.1 1.1 collective-permute-start.4
  15.2 15.8 %collective-permute-done = bf16[3,128,512]{2,1,0:T(8,128)(2,1)S(1)} collective-permute-done((bf16[3,128,512]{2,1,0:T(8,128)(2,1)}, bf16[3,128,512]{2,1,0:T(8,128)(2,1)S(1)}, u32[]{:S(2)}, u32[]{:S(2)}) %collective-permute-start) | collective-permute-done | bytes 393248 | tf_op jit(solution)/shard_map/ppermute | solution.py:23
  30.9 1.1 collective-permute-start.1
  32.0 15.8 %collective-permute-done.4 = bf16[3,128,512]{2,1,0:T(8,128)(2,1)S(1)} collective-permute-done((bf16[3,128,512]{2,1,0:T(8,128)(2,1)S(1)}, bf16[3,128,512]{2,1,0:T(8,128)(2,1)S(1)}, u32[]{:S(2)}, u32[]{:S(2)}) %collective-permute-start.4) | collective-permute-done | bytes 393248 | tf_op jit(solution)/shard_map/ppermute | solution.py:23
  48.7 1.3 copy.27
  50.0 5.5 %collective-permute-done.1 = bf16[3,128,512]{2,1,0:T(8,128)(2,1)} collective-permute-done((bf16[3,128,512]{2,1,0:T(8,128)(2,1)S(1)}, bf16[3,128,512]{2,1,0:T(8,128)(2,1)}, u32[]{:S(2)}, u32[]{:S(2)}) %collective-permute-start.1) | collective-permute-done | bytes 393248 | tf_op jit(solution)/shard_map/ppermute | solution.py:23
  55.5 1.3 pad_maximum_fusion
  57.7 0.8 copy-done.2
  59.1 1.3 fusion.54
  60.7 1.2 copy-done.3
  61.9 1.0 fusion.42
  62.9 0.9 copy.44
  63.8 3.5 %all-to-all-start.1 = ((bf16[4,128,512]{1,2,0:T(8,128)(2,1)}), bf16[4,128,512]{1,2,0:T(8,128)(2,1)S(1)}, u32[]{:S(2)}, u32[]{:S(2)}) async-start(bf16[4,128,512]{1,2,0:T(8,128)(2,1)} %bitcast.111), calls=%async_computation.1 | async-start | bytes 1048576 | tf_op jit(solution)/shard_map/all_to_all | solution.py:69
  67.6 0.7 all_to_all.30
  68.3 6.6 %all-to-all-done.1 = bf16[4,128,512]{1,2,0:T(8,128)(2,1)S(1)} async-done(((bf16[4,128,512]{1,2,0:T(8,128)(2,1)}), bf16[4,128,512]{1,2,0:T(8,128)(2,1)S(1)}, u32[]{:S(2)}, u32[]{:S(2)}) %all-to-all-start.1) | async-done | bytes 524320 | tf_op jit(solution)/shard_map/all_to_all | solution.py:69
  75.0 4.8 %all-to-all-start = ((s32[8,1,512]{2,1,0:T(1,128)}), s32[8,1,512]{2,1,0:T(1,128)S(1)}, u32[]{:S(2)}, u32[]{:S(2)}) async-start(s32[8,1,512]{2,1,0:T(1,128)} %all_to_all.30), calls=%async_computation | async-start | bytes 32768 | tf_op jit(solution)/shard_map/all_to_all | solution.py:96
  80.2 1.2 copy.31
  81.5 3.9 %all-to-all-done = s32[8,1,512]{2,1,0:T(1,128)S(1)} async-done(((s32[8,1,512]{2,1,0:T(1,128)}), s32[8,1,512]{2,1,0:T(1,128)S(1)}, u32[]{:S(2)}, u32[]{:S(2)}) %all-to-all-start) | async-done | bytes 16416 | tf_op jit(solution)/shard_map/all_to_all | solution.py:96
  85.4 3.6 %all-to-all-start.2 = ((bf16[8,128,512]{1,2,0:T(8,128)(2,1)}), bf16[8,128,512]{1,2,0:T(8,128)(2,1)S(1)}, u32[]{:S(2)}, u32[]{:S(2)}) async-start(bf16[8,128,512]{1,2,0:T(8,128)(2,1)} %bitcast.38), calls=%async_computation.2 | async-start | bytes 2097152 | tf_op jit(solution)/shard_map/all_to_all | solution.py:95
  89.0 26.5 %all-to-all-done.2 = bf16[8,128,512]{1,2,0:T(8,128)(2,1)S(1)} async-done(((bf16[8,128,512]{1,2,0:T(8,128)(2,1)}), bf16[8,128,512]{1,2,0:T(8,128)(2,1)S(1)}, u32[]{:S(2)}, u32[]{:S(2)}) %all-to-all-start.2) | async-done | bytes 1048608 | tf_op jit(solution)/shard_map/all_to_all | solution.py:95
  115.6 28.2 %scatter_custom_fusion = f32[8193,128]{1,0:T(8,128)} fusion(s32[4096]{0:T(1024)S(1)} %bitcast.127, f32[4096,128]{1,0:T(8,128)S(1)} %bitcast.115, f32[]{:T(128)} %constant.39.clone.1), kind=kCustom, calls=%fused_computation.4 | custom fusion | flops 524288 | bytes 4194820 | tf_op jit(solution)/shard_map/scatter-add | solution.py:100
  143.8 4.4 %slice_bitcast_fusion = f32[128,8192]{0,1:T(8,128)} fusion(f32[8193,128]{1,0:T(8,128)} %scatter_custom_fusion), kind=kLoop, calls=%fused_computation.3 | loop fusion | bytes 8388608 | tf_op jit(solution)/shard_map/transpose | solution.py:101
  148.3 5.6 %copy.32 = f32[128,8192]{1,0:T(8,128)} copy(f32[128,8192]{0,1:T(8,128)} %slice_bitcast_fusion) | data formatting | bytes 8388608 | tf_op jit(solution)/shard_map/transpose | solution.py:101
  (44 shorter events, 3.8 us)
Async XLA Ops:
  0.0 14.1 %collective-permute-start.3 = (bf16[3,128,512]{2,1,0:T(8,128)(2,1)}, bf16[3,128,512]{2,1,0:T(8,128)(2,1)S(1)}, u32[]{:S(2)}, u32[]{:S(2)}) collective-permute-start(bf16[3,128,512]{2,1,0:T(8,128)(2,1)} %param.11), channel_id=1, source_target_pairs={{0,8},{8,16},{16,24},{24,0},{1,9},{9,17},{17,25},{25,1},{2,10},{10... | collective-permute-start | bytes 1179656 | tf_op jit(solution)/shard_map/ppermute | solution.py:23
  3.0 29.1 %collective-permute-start.5 = (bf16[3,128,512]{2,1,0:T(8,128)(2,1)}, bf16[3,128,512]{2,1,0:T(8,128)(2,1)S(1)}, u32[]{:S(2)}, u32[]{:S(2)}) collective-permute-start(bf16[3,128,512]{2,1,0:T(8,128)(2,1)} %param.11), channel_id=1, source_target_pairs={{8,0},{16,8},{24,16},{0,24},{9,1},{17,9},{25,17},{1,25},{10,2},{18... | collective-permute-start | bytes 1179656 | tf_op jit(solution)/shard_map/ppermute | solution.py:25
  3.9 27.0 %collective-permute-start = (bf16[3,128,512]{2,1,0:T(8,128)(2,1)}, bf16[3,128,512]{2,1,0:T(8,128)(2,1)S(1)}, u32[]{:S(2)}, u32[]{:S(2)}) collective-permute-start(bf16[3,128,512]{2,1,0:T(8,128)(2,1)} %param.12), channel_id=1, source_target_pairs={{0,8},{8,16},{16,24},{24,0},{1,9},{9,17},{17,25},{25,1},{2,10},{10... | collective-permute-start | bytes 1179656 | tf_op jit(solution)/shard_map/ppermute | solution.py:23
  5.0 45.0 %collective-permute-start.2 = (bf16[3,128,512]{2,1,0:T(8,128)(2,1)}, bf16[3,128,512]{2,1,0:T(8,128)(2,1)}, u32[]{:S(2)}, u32[]{:S(2)}) collective-permute-start(bf16[3,128,512]{2,1,0:T(8,128)(2,1)} %param.12), channel_id=1, source_target_pairs={{8,0},{16,8},{24,16},{0,24},{9,1},{17,9},{25,17},{1,25},{10,2},{18... | collective-permute-start | bytes 1179656 | tf_op jit(solution)/shard_map/ppermute | solution.py:25
  9.8 3.0 %copy-start = (bf16[1,512,512]{2,1,0:T(8,128)(2,1)S(1)}, bf16[1,512,512]{2,1,0:T(8,128)(2,1)}, u32[]{:S(2)}) copy-start(bf16[1,512,512]{2,1,0:T(8,128)(2,1)} %param.10) | copy-start | bytes 1572868
  9.8 3.0 %copy-start.1 = (bf16[1,512,512]{2,1,0:T(8,128)(2,1)S(1)}, bf16[1,512,512]{2,1,0:T(8,128)(2,1)}, u32[]{:S(2)}) copy-start(bf16[1,512,512]{2,1,0:T(8,128)(2,1)} %param.8) | copy-start | bytes 1572868
  11.5 20.5 %copy-start.9 = (s32[2048]{0:T(1024)S(1)}, s32[2048]{0:T(1024)}, u32[]{:S(2)}) copy-start(s32[2048]{0:T(1024)} %param.14) | copy-start | bytes 24580
  11.5 36.3 %copy-start.7 = (bf16[3,128,512]{2,1,0:T(8,128)(2,1)S(1)}, bf16[3,128,512]{2,1,0:T(8,128)(2,1)}, u32[]{:S(2)}) copy-start(bf16[3,128,512]{2,1,0:T(8,128)(2,1)} %param.11) | copy-start | bytes 1179652
  14.1 33.7 %collective-permute-start.4 = (bf16[3,128,512]{2,1,0:T(8,128)(2,1)S(1)}, bf16[3,128,512]{2,1,0:T(8,128)(2,1)S(1)}, u32[]{:S(2)}, u32[]{:S(2)}) collective-permute-start(bf16[3,128,512]{2,1,0:T(8,128)(2,1)S(1)} %collective-permute-done.3), channel_id=1, source_target_pairs={{0,8},{8,16},{16,24},{24,0},{1,9},{9,17},{17,25},{25,1},{2,10},{10... | collective-permute-start | bytes 1179656 | tf_op jit(solution)/shard_map/ppermute | solution.py:23
  30.9 24.5 %collective-permute-start.1 = (bf16[3,128,512]{2,1,0:T(8,128)(2,1)S(1)}, bf16[3,128,512]{2,1,0:T(8,128)(2,1)}, u32[]{:S(2)}, u32[]{:S(2)}) collective-permute-start(bf16[3,128,512]{2,1,0:T(8,128)(2,1)S(1)} %collective-permute-done), channel_id=1, source_target_pairs={{0,8},{8,16},{16,24},{24,0},{1,9},{9,17},{17,25},{25,1},{2,10},{10... | collective-permute-start | bytes 1179656 | tf_op jit(solution)/shard_map/ppermute | solution.py:23
  48.7 6.8 %copy-start.8 = (bf16[3,128,512]{2,1,0:T(8,128)(2,1)S(1)}, bf16[3,128,512]{2,1,0:T(8,128)(2,1)}, u32[]{:S(2)}) copy-start(bf16[3,128,512]{2,1,0:T(8,128)(2,1)} %param.12) | copy-start | bytes 1179652
  57.5 1.0 copy-start.2
  57.5 1.2 copy-start.4
  57.5 1.3 copy-start.5
  57.5 1.5 copy-start.6
  57.5 1.6 %copy-start.12 = (bf16[1,512,512]{2,1,0:T(8,128)(2,1)S(1)}, bf16[1,512,512]{2,1,0:T(8,128)(2,1)}, u32[]{:S(2)}) copy-start(bf16[1,512,512]{2,1,0:T(8,128)(2,1)} %param.9) | copy-start | bytes 1572868
  60.4 1.4 copy-start.3
  62.9 4.4 %copy-start.10 = (s32[64,1]{0,1:T(1,128)S(1)}, s32[64,1]{0,1:T(1,128)}, u32[]{:S(2)}) copy-start(s32[64,1]{0,1:T(1,128)} %param.15) | copy-start | bytes 772
  62.9 4.4 %copy-start.11 = (s32[64]{0:T(128)S(1)}, s32[64]{0:T(128)}, u32[]{:S(2)}) copy-start(s32[64]{0:T(128)} %select_reduce_fusion) | copy-start | bytes 772
  63.8 11.2 %all-to-all-start.1 = ((bf16[4,128,512]{1,2,0:T(8,128)(2,1)}), bf16[4,128,512]{1,2,0:T(8,128)(2,1)S(1)}, u32[]{:S(2)}, u32[]{:S(2)}) async-start(bf16[4,128,512]{1,2,0:T(8,128)(2,1)} %bitcast.111), calls=%async_computation.1 | async-start | bytes 1048576 | tf_op jit(solution)/shard_map/all_to_all | solution.py:69
  75.0 10.4 %all-to-all-start = ((s32[8,1,512]{2,1,0:T(1,128)}), s32[8,1,512]{2,1,0:T(1,128)S(1)}, u32[]{:S(2)}, u32[]{:S(2)}) async-start(s32[8,1,512]{2,1,0:T(1,128)} %all_to_all.30), calls=%async_computation | async-start | bytes 32768 | tf_op jit(solution)/shard_map/all_to_all | solution.py:96
  85.4 30.1 %all-to-all-start.2 = ((bf16[8,128,512]{1,2,0:T(8,128)(2,1)}), bf16[8,128,512]{1,2,0:T(8,128)(2,1)S(1)}, u32[]{:S(2)}, u32[]{:S(2)}) async-start(bf16[8,128,512]{1,2,0:T(8,128)(2,1)} %bitcast.38), calls=%async_computation.2 | async-start | bytes 2097152 | tf_op jit(solution)/shard_map/all_to_all | solution.py:95
